TPU v7x, 32 devices: a whole 2x2x4 slice. The times are simulated.
32 devices in a mesh: seq: 4 (over y, x), tp: 8 (over z, core).
Axes of the slice: x: 2, y: 2, z: 4, core: 2. Of those that a mesh axis runs over, the one named last changes fastest.
Arguments:
- hidden: bfloat16 [4096, 4096], P(('seq', 'tp')), may hold values from -6 to 6
- norm_gain: float32 [4096], replicated, may hold values from 0.5 to 1.5
- inner_weight: bfloat16 [4096, 2, 2048], P(None, None, 'tp'), may hold values from -0.09375 to 0.09375
- group_weight: bfloat16 [4096, 1024], P(None, 'tp'), may hold values from -0.09375 to 0.09375
- step_weight: bfloat16 [4096, 32], P(None, 'tp'), may hold values from -0.09375 to 0.09375
- step_bias: float32 [32], P('tp'), may hold values from -2 to 1
- decay_rate: float32 [32], P('tp'), may hold values from 0.0001 to 0.1
- filter_inner: bfloat16 [4, 2048], P(None, 'tp'), may hold values from -3 to 3
- filter_group: bfloat16 [4, 1024], P(None, 'tp'), may hold values from -3 to 3
- skip_gain: float32 [32], P('tp'), may hold values from 0.5 to 1.5
- mixer_gain: float32 [2048], P('tp'), may hold values from 0.5 to 1.5
- output_weight: bfloat16 [2048, 4096], P('tp'), may hold values from -0.125 to 0.125
- segment_ids: int32 [4096], replicated, may hold values from 0 to 3, never falling along the last dimension, each value on 1 to 2048 neighbouring positions
Outputs:
- layer_out: bfloat16 [4096, 4096], P(('seq', 'tp'))
Inputs may be any that keep to these rules, and one draw needn't show every extreme that they name: `segment_ids`: ids never fall along the pack; every id names at least one token, and one request has exactly 2048 tokens.
All inputs are finite; a program needn't handle non-finite values.
Results may differ from a plain program's by a relative error of at most 0.0051.
Values may be sent and summed in bfloat16 or wider, within the bound.
A program may use at most 128 MiB of HBM per device.

v0:
```python
import jax
import jax.numpy as jnp
from jax import lax
from jax.sharding import PartitionSpec as P

STRETCH = 256
EPS = 1e-05
HIGH = lax.Precision.HIGHEST


def swapped(block, axis, stride):
    count = lax.axis_size(axis)
    route = []
    for low in range(count):
        high = low | 1 << stride
        if high != low and high < count:
            route += [(low, high), (high, low)]
    return lax.ppermute(block, axis, route)


def from_behind(array, axis, by):
    size = lax.axis_size(axis)
    pairs = [(i, i + by) for i in range(size) if 0 <= i + by < size]
    return lax.ppermute(array, axis, pairs)


def entering_2(value, axis, join, neutral):
    count, mine = (lax.axis_size(axis), lax.axis_index(axis))
    pieces = jax.tree.map(lambda part: lax.all_gather(part, axis), value)
    total = jax.tree.map(
        lambda part, zero: jnp.full_like(part, 0) + jnp.asarray(zero, part.dtype), value, neutral
    )

    def hop(position, total):
        longer = join(total, jax.tree.map(lambda part: part[position], pieces))
        return jax.tree.map(lambda new, old: jnp.where(position < mine, new, old), longer, total)

    return lax.fori_loop(0, count - 1, hop, total)


def combine(earlier, later):
    return (earlier[0] * later[0], later[0][:, None, None] * earlier[1] + later[1])


def body(
    hidden,
    norm_gain,
    inner_weight,
    group_weight,
    step_weight,
    step_bias,
    decay_rate,
    filter_inner,
    filter_group,
    skip_gain,
    mixer_gain,
    output_weight,
    segment_ids,
):
    rows = hidden.shape[0]
    length = rows * lax.axis_size("tp")
    width = hidden.shape[1]
    inner_dev = inner_weight.shape[2]
    heads_dev = step_weight.shape[1]
    head_dim = inner_dev // heads_dev
    state_dim = group_weight.shape[1]
    taps = filter_inner.shape[0]
    first_row = lax.axis_index("seq") * length
    is_first = lax.axis_index("tp") % 2 == 0
    hidden_f = hidden.astype(jnp.float32)
    normed = (
        hidden_f
        * lax.rsqrt(jnp.mean(hidden_f * hidden_f, axis=-1, keepdims=True) + EPS)
        * norm_gain
    ).astype(jnp.bfloat16)
    other_weight, other_filter = swapped((group_weight, filter_group), "tp", 0)
    group_cols = (
        jnp.where(is_first, group_weight, other_weight),
        jnp.where(is_first, other_weight, group_weight),
    )
    filters = jnp.concatenate(
        [
            filter_inner,
            jnp.where(is_first, filter_group, other_filter),
            jnp.where(is_first, other_filter, filter_group),
        ],
        axis=1,
    )
    matrices = (inner_weight.reshape(width, 2 * inner_dev),) + group_cols + (step_weight,)
    piece = lax.all_gather(normed, "tp", axis=0, tiled=True)
    projected = jnp.concatenate(
        [jnp.dot(piece, matrix, preferred_element_type=jnp.float32) for matrix in matrices], axis=1
    )
    gate_z = projected[:, :inner_dev]
    conv_in = projected[:, inner_dev:-heads_dev]
    step_raw = projected[:, -heads_dev:]
    seg_pad = jnp.concatenate([jnp.full((taps - 1,), -1, jnp.int32), segment_ids])
    seg_ext = lax.dynamic_slice_in_dim(seg_pad, first_row, length + taps - 1)
    seg_local = seg_ext[taps - 1 :]
    before = from_behind(conv_in[length - (taps - 1) :], "seq", 1)
    extended = jnp.concatenate([before, conv_in], axis=0)
    filters_f = filters.astype(jnp.float32)
    total = jnp.zeros_like(conv_in)
    for offset in range(taps):
        same = (seg_ext[offset : offset + length] == seg_local).astype(jnp.float32)
        total = total + filters_f[offset] * extended[offset : offset + length] * same[:, None]
    active = jax.nn.silu(total)
    inner_x = active[:, :inner_dev]
    input_map = active[:, inner_dev : inner_dev + state_dim]
    output_map = active[:, inner_dev + state_dim :]
    starts = seg_local != seg_ext[taps - 2 : taps - 2 + length]
    step = jax.nn.softplus(step_raw + step_bias)
    log_decay = -step * decay_rate
    blocks = length // STRETCH
    block_x = inner_x.reshape(blocks, STRETCH, heads_dev, head_dim)
    block_b = input_map.reshape(blocks, STRETCH, state_dim)
    block_c = output_map.reshape(blocks, STRETCH, state_dim)
    step_heads = step.reshape(blocks, STRETCH, heads_dev).transpose(0, 2, 1)
    cumul = jnp.cumsum(log_decay.reshape(blocks, STRETCH, heads_dev), axis=1).transpose(0, 2, 1)
    block_seg = seg_local.reshape(blocks, STRETCH)
    block_start = starts.reshape(blocks, STRETCH)
    causal = jnp.tril(jnp.ones((STRETCH, STRETCH), jnp.bool_))
    same_seg = ((block_seg[:, :, None] == block_seg[:, None, :]) & causal)[:, None]
    gaps = cumul[:, :, :, None] - cumul[:, :, None, :]
    decay = jnp.where(same_seg, jnp.exp(jnp.where(same_seg, gaps, 0.0)), 0.0)
    products = jnp.einsum("cin,cjn->cij", block_c, block_b, precision=HIGH)
    mixing = decay * products[:, None] * step_heads[:, :, None, :]
    local_y = jnp.einsum("chij,cjhp->cihp", mixing, block_x, precision=HIGH)
    same_last = (block_seg == block_seg[:, -1:])[:, None, :]
    last_gap = cumul[:, :, -1:] - cumul
    end_weight = (
        jnp.where(same_last, jnp.exp(jnp.where(same_last, last_gap, 0.0)), 0.0) * step_heads
    )
    block_state = jnp.einsum("chj,cjhp,cjn->chpn", end_weight, block_x, block_b, precision=HIGH)
    clean = jnp.logical_not(jnp.any(block_start, axis=1)).astype(jnp.float32)
    block_keep = jnp.exp(cumul[:, :, -1]) * clean[:, None]

    def carry_blocks(carry, inputs):
        acc_state, acc_keep = carry
        keep, fresh = inputs
        return ((keep[:, None, None] * acc_state + fresh, acc_keep * keep), (acc_state, acc_keep))

    empty_state = jnp.zeros((heads_dev, head_dim, state_dim), jnp.float32)
    unit_keep = jnp.ones((heads_dev,), jnp.float32)
    (device_state, device_keep), (prior_state, prior_keep) = lax.scan(
        carry_blocks, (empty_state, unit_keep), (block_keep, block_state)
    )
    entering = entering_2((device_keep, device_state), "seq", combine, (unit_keep, empty_state))
    incoming = entering[1]
    entry_state = prior_state + prior_keep[:, :, None, None] * incoming[None]
    alive = (jnp.cumsum(block_start.astype(jnp.int32), axis=1) == 0).astype(jnp.float32)
    entry_weight = jnp.exp(cumul) * alive[:, None, :]
    carried_y = jnp.einsum("chi,cin,chpn->cihp", entry_weight, block_c, entry_state, precision=HIGH)
    ssm_out = (local_y + carried_y).reshape(length, heads_dev, head_dim) + skip_gain[
        None, :, None
    ] * inner_x.reshape(length, heads_dev, head_dim)
    gated = ssm_out.reshape(length, inner_dev) * jax.nn.silu(gate_z)
    own_squares = jnp.sum(gated * gated, axis=-1)
    other_squares = swapped(own_squares, "tp", 0)
    group_mean = (own_squares + other_squares) / (2 * inner_dev)
    mixed = (gated * lax.rsqrt(group_mean + EPS)[:, None] * mixer_gain).astype(jnp.bfloat16)
    partial_out = jnp.dot(mixed, output_weight, preferred_element_type=jnp.float32)
    mine = lax.psum_scatter(partial_out, "tp", scatter_dimension=0, tiled=True)
    return (hidden_f + mine).astype(jnp.bfloat16)


def solution(mesh):
    in_specs = (
        P(("seq", "tp"), None),
        P(),
        P(None, None, "tp"),
        P(None, "tp"),
        P(None, "tp"),
        P("tp"),
        P("tp"),
        P(None, "tp"),
        P(None, "tp"),
        P("tp"),
        P("tp"),
        P("tp", None),
        P(),
    )
    out_specs = P(("seq", "tp"), None)
    return jax.shard_map(body, mesh=mesh, in_specs=in_specs, out_specs=out_specs, check_vma=False)
```

profile of v0, /device:TPU:0, one launch (start us, length us, event | category | flops | bytes accessed | tf_op | source)
XLA Modules:
  0.0 372.5 jit_solution(9451892559120451516)
XLA Ops:
  6.6 1.7 fusion.20
  8.3 2.5 fusion.22
  11.6 1.2 reduce-window.16
  14.8 4.9 %copy.92 = bf16[512,8,2,256]{3,1,2,0:T(8,128)(2,1)} copy(bf16[512,8,2,256]{3,2,1,0:T(2,128)(2,1)} %bitcast.91) | data formatting | bytes 8388608
  21.1 74.7 %all-gather.4.cloned.1.call-done = bf16[1024,4096]{1,0:T(8,128)(2,1)} async-done(((bf16[128,4096]{1,0:T(8,128)(2,1)}), bf16[1024,4096]{1,0:T(8,128)(2,1)}) %all-gather.4.cloned.1.call-update) | async-done | bytes 8388624 | tf_op jit(solution)/shard_map/all_gather | solution.py:90
  95.8 5.7 %negate_multiply_fusion = (f32[1024,4]{0,1:T(4,128)S(1)}, f32[1024,4]{0,1:T(4,128)S(1)}) fusion(f32[4]{0:T(128)S(1)} %copy-done.15, f32[4]{0:T(128)S(1)} %copy-done.16, bf16[1024,4096]{1,0:T(8,128)(2,1)} %all-gather.4.cloned.1.call-done, bf16[4096,4]{0,1:T(4,128)(2,1)S(1)} %copy-done.13), kind=kOutput, calls=%fused_computation.96 | convolution fusion | flops 33591296 | bytes 8454176 | tf_op jit(solution)/shard_map/dot_general | solution.py:92
  101.5 4.8 %reduce-window.14 = f32[4,4,2,128]{3,2,1,0:T(2,128)S(1)} reduce-window(f32[4,4,2,128]{3,2,1,0:T(2,128)S(1)} %copy.83, f32[]{:T(128)} %constant.89.clone.1), window={size=1x1x1x128 pad=0_0x0_0x0_0x127_0}, to_apply=%region_1.2 | reduce-window | flops 520192 | bytes 32772 | tf_op jit(solution)/shard_map/reduce-window
  107.2 6.7 %fusion.38 = f32[1024,128]{0,1:T(8,128)S(1)} fusion(bf16[1024,4096]{1,0:T(8,128)(2,1)} %all-gather.4.cloned.1.call-done, bf16[4096,128]{1,0:T(8,128)(2,1)} %collective-permute-done.1, bf16[4096,128]{1,0:T(8,128)(2,1)S(1)} %copy-done.7, pred[]{:T(512)S(6)} %eq.59), kind=kOutput, calls=%fused_computation.58 | convolution fusion | flops 1074266112 | bytes 11010049 | tf_op jit(solution)/shard_map/dot_general | solution.py:92
  113.8 2.9 fusion.40
  116.8 6.5 %fusion.78 = f32[1024,512]{0,1:T(8,128)S(1)} fusion(bf16[1024,4096]{1,0:T(8,128)(2,1)S(1)} %copy-done.1, bf16[4096,512]{1,0:T(8,128)(2,1)} %bitcast.92), kind=kOutput, calls=%fused_computation.123 | convolution fusion | flops 4294967296 | bytes 14680064 | tf_op jit(solution)/shard_map/dot_general | solution.py:92
  123.4 3.6 collective-permute-start.2
  127.4 5.9 %collective-permute-done.2 = f32[3,512]{0,1:T(8,128)S(1)} collective-permute-done((f32[3,512]{0,1:T(8,128)S(1)}, f32[3,512]{0,1:T(8,128)S(1)}, u32[]{:S(2)}, u32[]{:S(2)}) %collective-permute-start.2) | collective-permute-done | bytes 6176 | tf_op jit(solution)/shard_map/ppermute | solution.py:24
  133.3 2.4 divide_multiply_fusion
  135.7 1.1 slice.107
  137.4 2.7 reshape.145
  140.1 1.0 reshape.150
  141.1 3.4 fusion.36
  144.5 6.9 %while.31 = (s32[]{:T(128)}, f32[4,64,128]{2,1,0:T(8,128)S(1)}, f32[4]{0:T(128)S(1)}, f32[4,4,64,128]{3,2,1,0:T(8,128)}, f32[4,4]{1,0:T(4,128)S(1)}, /*index=5*/...) while((s32[]{:T(128)}, f32[4,64,128]{2,1,0:T(8,128)S(1)}, f32[4]{0:T(128)S(1)}, ...), condition=%wide.region_7.8_spmd.clone, body=%wide.region_6.7_spmd.clone.sunk | while | flops 131083 | bytes 655617 | solution.py:145
  151.6 1.0 reshape.149
  152.7 10.8 %all-reduce.1 = f32[16]{0:T(128)S(1)} all-reduce(f32[16]{0:T(128)S(1)} %dynamic-update-slice), channel_id=2, replica_groups=mesh['seq'=4,'tp'=8] {'seq'}, use_global_device_ids=true, to_apply=%add.1 | all-reduce | flops 16 | bytes 128
  163.6 10.2 %all-gather.1 = f32[16,64,128]{2,1,0:T(8,128)} all-gather(f32[4,64,128]{2,1,0:T(8,128)S(1)} %get-tuple-element.142), channel_id=3, replica_groups=mesh['seq'=4,'tp'=8] {'seq'}, dimensions={0}, use_global_device_ids=true | all-gather | bytes 655360 | tf_op jit(solution)/shard_map/all_gather | solution.py:29
  173.8 3.1 while.32
  173.8 1.0 fusion.89
  174.9 1.0 fusion.89
  175.9 1.0 fusion.89
  176.9 1.0 fusion.47
  178.2 5.2 %fusion.33 = f32[4,256,4,64]{1,3,2,0:T(8,128)S(1)} fusion(f32[4,4,256]{2,1,0:T(4,128)S(1)} %copy.69, f32[4,256,256]{2,1,0:T(8,128)S(1)} %fusion.47, f32[4,4,256]{2,1,0:T(4,128)S(1)} %reduce_window_sum.41, pred[4,256,256]{2,1,0:T(8,128)(4,1)S(1)} %copy-done.11, f32[4,256,4,64]{1,0,3,2:T(4,128)S(1)} %copy-done.8), kind=kOutput, calls=%fused_computation.51 | convolution fusion | flops 810549248 | bytes 3440640 | tf_op jit(solution)/shard_map/chij,cjhp->cihp/dot_general | solution.py:128
  183.4 1.1 fusion.32
  187.3 1.2 collective-permute-done.3
  188.4 8.2 %fusion.46 = f32[1024,4096]{1,0:T(8,128)} fusion(bf16[256,4096]{1,0:T(8,128)(2,1)S(1)} %copy-done, f32[1024,256]{0,1:T(8,128)S(1)} %get-tuple-element.213, f32[256]{0:T(256)S(1)} %copy-done.14, f32[1024]{0:T(1024)S(1)} %add_rsqrt_fusion), kind=kOutput, calls=%fused_computation.67 | convolution fusion | flops 2148270080 | bytes 19928064 | tf_op jit(solution)/shard_map/dot_general | solution.py:162
  196.7 166.2 %reduce-scatter.2.cloned.1.call-done = f32[128,4096]{1,0:T(8,128)} async-done(((f32[1024,4096]{1,0:T(8,128)}), f32[128,4096]{1,0:T(8,128)}) %reduce-scatter.2.cloned.1.call-update) | async-done | bytes 2097168 | tf_op jit(solution)/shard_map/reduce_scatter | solution.py:163
  362.8 2.8 fusion.23
  (127 shorter events, 15.4 us)
Async XLA Ops:
  6.5 181.9 %copy-start = (bf16[256,4096]{1,0:T(8,128)(2,1)S(1)}, bf16[256,4096]{1,0:T(8,128)(2,1)}, u32[]{:S(2)}) copy-start(bf16[256,4096]{1,0:T(8,128)(2,1)} %param.28) | copy-start | bytes 6291460
  6.5 4.3 %copy-start.18 = (bf16[4,128]{1,0:T(4,128)(2,1)S(1)}, bf16[4,128]{1,0:T(4,128)(2,1)}, u32[]{:S(2)}) copy-start(bf16[4,128]{1,0:T(4,128)(2,1)} %param.25) | copy-start | bytes 3076
  6.5 4.9 %copy-start.7 = (bf16[4096,128]{1,0:T(8,128)(2,1)S(1)}, bf16[4096,128]{1,0:T(8,128)(2,1)}, u32[]{:S(2)}) copy-start(bf16[4096,128]{1,0:T(8,128)(2,1)} %param.20) | copy-start | bytes 3145732
  6.5 5.0 %copy-start.12 = (s32[4096]{0:T(1024)S(1)}, s32[4096]{0:T(1024)}, u32[]{:S(2)}) copy-start(s32[4096]{0:T(1024)} %param.29) | copy-start | bytes 49156
  6.5 89.2 %all-gather.4.cloned.1.call-start = ((), (), s32[]{:S(2)}) async-start(), calls=%async_computation.1 | async-start | bytes 9437184 | tf_op jit(solution)/shard_map/all_gather | solution.py:90
  8.3 6.3 %copy-start.19 = (f32[4]{0:T(128)S(1)}, f32[4]{0:T(128)}, u32[]{:S(2)}) copy-start(f32[4]{0:T(128)} %param.26) | copy-start | bytes 52
  10.8 352.0 %reduce-scatter.2.cloned.1.call-start = ((), (), s32[]{:S(2)}) async-start(), calls=%async_computation.2 | async-start | bytes 18874368 | tf_op jit(solution)/shard_map/reduce_scatter | solution.py:163
  10.9 10.1 %collective-permute-start = (bf16[4,128]{1,0:T(4,128)(2,1)S(1)}, bf16[4,128]{1,0:T(4,128)(2,1)S(1)}, u32[]{:S(2)}, u32[]{:S(2)}) collective-permute-start(bf16[4,128]{1,0:T(4,128)(2,1)S(1)} %copy-done.18), channel_id=1, source_target_pairs={{0,1},{1,0},{2,3},{3,2},{4,5},{5,4},{6,7},{7,6},{8,9},{9,8},{10,11... | collective-permute-start | bytes 3080 | tf_op jit(solution)/shard_map/ppermute | solution.py:18
  11.4 95.7 %collective-permute-start.1 = (bf16[4096,128]{1,0:T(8,128)(2,1)S(1)}, bf16[4096,128]{1,0:T(8,128)(2,1)}, u32[]{:S(2)}, u32[]{:S(2)}) collective-permute-start(bf16[4096,128]{1,0:T(8,128)(2,1)S(1)} %copy-done.7), channel_id=1, source_target_pairs={{0,1},{1,0},{2,3},{3,2},{4,5},{5,4},{6,7},{7,6},{8,9},{9,8},{10,11... | collective-permute-start | bytes 3145736 | tf_op jit(solution)/shard_map/ppermute | solution.py:18
  14.8 5.0 %copy-start.20 = (u32[32]{0:T(128)S(1)}, u32[32]{0:T(128)}, u32[]{:S(2)}) copy-start(u32[32]{0:T(128)} %constant.107) | copy-start | bytes 388
  14.8 6.3 %copy-start.17 = (bf16[4,256]{1,0:T(4,128)(2,1)S(1)}, bf16[4,256]{1,0:T(4,128)(2,1)}, u32[]{:S(2)}) copy-start(bf16[4,256]{1,0:T(4,128)(2,1)} %param.24) | copy-start | bytes 6148
  14.8 81.0 %copy-start.13 = (bf16[4096,4]{0,1:T(4,128)(2,1)S(1)}, bf16[4096,4]{0,1:T(4,128)(2,1)}, u32[]{:S(2)}) copy-start(bf16[4096,4]{0,1:T(4,128)(2,1)} %param.21) | copy-start | bytes 98308
  14.8 81.0 %copy-start.15 = (f32[4]{0:T(128)S(1)}, f32[4]{0:T(128)}, u32[]{:S(2)}) copy-start(f32[4]{0:T(128)} %param.23) | copy-start | bytes 52
  14.8 81.0 %copy-start.16 = (f32[4]{0:T(128)S(1)}, f32[4]{0:T(128)}, u32[]{:S(2)}) copy-start(f32[4]{0:T(128)} %param.22) | copy-start | bytes 52
  107.1 6.7 %copy-start.1 = (bf16[1024,4096]{1,0:T(8,128)(2,1)S(1)}, bf16[1024,4096]{1,0:T(8,128)(2,1)}, u32[]{:S(2)}) copy-start(bf16[1024,4096]{1,0:T(8,128)(2,1)} %all-gather.4.cloned.1.call-done) | copy-start | bytes 25165828
  123.3 4.1 %copy-start.4 = (f32[1024,512]{0,1:T(8,128)}, f32[1024,512]{0,1:T(8,128)S(1)}, u32[]{:S(2)}) copy-start(f32[1024,512]{0,1:T(8,128)S(1)} %fusion.78) | copy-start | bytes 6291460
  123.4 9.8 %collective-permute-start.2 = (f32[3,512]{0,1:T(8,128)S(1)}, f32[3,512]{0,1:T(8,128)S(1)}, u32[]{:S(2)}, u32[]{:S(2)}) collective-permute-start(f32[3,512]{0,1:T(8,128)S(1)} %pad_maximum_fusion.3), channel_id=1, source_target_pairs={{0,8},{8,16},{16,24},{1,9},{9,17},{17,25},{2,10},{10,18},{18,26},{... | collective-permute-start | bytes 18440 | tf_op jit(solution)/shard_map/ppermute | solution.py:24
  135.6 1.6 copy-start.2
  176.9 1.2 copy-start.8
  176.9 1.3 copy-start.11
  178.2 5.2 %copy-start.9 = (f32[4,256,128]{1,0,2:T(4,128)S(1)}, f32[4,256,128]{1,0,2:T(4,128)}, u32[]{:S(2)}) copy-start(f32[4,256,128]{1,0,2:T(4,128)} %reshape.149) | copy-start | bytes 1572868
  178.2 5.2 %copy-start.10 = (f32[4,4,64,128]{3,2,1,0:T(8,128)S(1)}, f32[4,4,64,128]{3,2,1,0:T(8,128)}, u32[]{:S(2)}) copy-start(f32[4,4,64,128]{3,2,1,0:T(8,128)} %get-tuple-element.139) | copy-start | bytes 1572868
  184.5 1.6 copy-start.3
  184.6 2.2 copy-start.5
  186.8 1.7 copy-start.14
  187.2 1.2 collective-permute-start.3
  196.7 166.2 %copy-start.6 = (bf16[128,4096]{1,0:T(8,128)(2,1)S(1)}, bf16[128,4096]{1,0:T(8,128)(2,1)}, u32[]{:S(2)}) copy-start(bf16[128,4096]{1,0:T(8,128)(2,1)} %param.17) | copy-start | bytes 3145732
Sparse Core Ops, SparseCore 0:
  10.9 84.7 all-gather.3
  196.8 165.9 reduce-scatter.1
where the time goes:
time: 373 us; the launch traced here: 372 us
  waiting for transfers between devices  248 us (66%)
  matrix products  40.7 us (11%)
  other arithmetic  27.4 us (7%)
  blocking collectives  21.1 us (6%)
  local copies, waits for them, and re-layouts  16.4 us (4%)
  between operations  14.5 us (4%)
  starting transfers between devices  4.37 us (1%)
    reduce_scatter x1, waiting for transfers between devices, body(): mine = lax.psum_scatter(partial_out, 'tp', scatter_dimension=0, tiled=True)  166 us
    all_gather x1, waiting for transfers between devices, body(): piece = lax.all_gather(normed, 'tp', axis=0, tiled=True)  74.7 us
    dot_general x4, matrix products, body(): jnp.dot(piece, matrix, preferred_element_type=jnp.float32)  21.8 us
    unnamed x1, blocking collectives  10.8 us
    all_gather x1, blocking collectives, entering_2(): pieces = jax.tree.map(lambda part: lax.all_gather(part, axis), value)  10.2 us
    unnamed x49, local copies, waits for them, and re-layouts  8.25 us
    dot_general x1, matrix products, body(): jnp.dot(mixed, output_weight, preferred_element_type=jnp.float32)  8.21 us
  transfers between devices with their start and end apart: 6, of which 4 were waited for; matrix products, arithmetic and copies ran while one was open for 5% of the time, Pallas kernels for 0%

commit v1 on v0

--- a/solution.py
+++ b/solution.py
@@ -87,7 +87,12 @@
         axis=1,
     )
     matrices = (inner_weight.reshape(width, 2 * inner_dev),) + group_cols + (step_weight,)
-    piece = lax.all_gather(normed, "tp", axis=0, tiled=True)
+    ring = [normed]
+    for hop_ in range(7):
+        ring.append(lax.ppermute(ring[-1], "tp", [(dev, (dev + 1) % 8) for dev in range(8)]))
+    piece = jnp.roll(
+        jnp.concatenate(ring[::-1], axis=0), (lax.axis_index("tp") + 1) * ring[0].shape[0], axis=0
+    )
     projected = jnp.concatenate(
         [jnp.dot(piece, matrix, preferred_element_type=jnp.float32) for matrix in matrices], axis=1
     )

time: 373 us -> 435 us (1.17)
  local copies, waits for them, and re-layouts: 16.4 us -> 47.9 us
  waiting for transfers between devices: 248 us -> 269 us
  matrix products: 40.7 us -> 45.7 us
    ppermute x0 -> x7, waiting for transfers between devices: none -> 101 us  [body(): lax.ppermute(ring[-1], 'tp', [(dev, (dev + 1) % 8) for dev in range(8)])]
    all_gather x1 -> x0, waiting for transfers between devices: 74.7 us -> none  [body(): piece = lax.all_gather(normed, 'tp', axis=0, tiled=True)]
    unnamed x49 -> x85, local copies, waits for them, and re-layouts: 8.25 us -> 25.8 us
    dynamic_update_slice x4, local copies, waits for them, and re-layouts: 0.16 us -> 4.97 us  [body(): lax.scan(carry_blocks, (empty_state, unit_keep), (block_keep, block_state))]
  transfers between devices with their start and end apart: 6 -> 12, of which waited for: 4 -> 10; matrix products, arithmetic and copies ran while one was open for 5% -> 9% of each run, Pallas kernels for 0% -> 0%
where the time goes in v1:
time: 435 us; the launch traced here: 434 us
  waiting for transfers between devices  269 us (62%)
  local copies, waits for them, and re-layouts  47.9 us (11%)
  matrix products  45.7 us (11%)
  other arithmetic  29.2 us (7%)
  blocking collectives  22.2 us (5%)
  between operations  14.8 us (3%)
  starting transfers between devices  5.19 us (1%)
    reduce_scatter x1, waiting for transfers between devices, body(): mine = lax.psum_scatter(partial_out, 'tp', scatter_dimension=0, tiled=True)  165 us
    ppermute x7, waiting for transfers between devices, body(): lax.ppermute(ring[-1], 'tp', [(dev, (dev + 1) % 8) for dev in range(8)])  101 us
    unnamed x85, local copies, waits for them, and re-layouts  25.8 us
    dot_general x4, matrix products, body(): jnp.dot(piece, matrix, preferred_element_type=jnp.float32)  24.2 us
    all_gather x1, blocking collectives, entering_2(): pieces = jax.tree.map(lambda part: lax.all_gather(part, axis), value)  12.6 us
    unnamed x1, blocking collectives  9.62 us
  transfers between devices with their start and end apart: 12, of which 10 were waited for; matrix products, arithmetic and copies ran while one was open for 9% of the time, Pallas kernels for 0%

profile of v1, /device:TPU:0, one launch (start us, length us, event | category | flops | bytes accessed | tf_op | source)
XLA Modules:
  0.0 434.2 jit_solution(1382030679393940975)
XLA Ops:
  6.5 1.7 fusion.28
  8.2 1.6 fusion.30
  10.3 16.5 %collective-permute-done.1 = bf16[128,4096]{1,0:T(8,128)(2,1)S(1)} collective-permute-done((bf16[128,4096]{1,0:T(8,128)(2,1)S(1)}, bf16[128,4096]{1,0:T(8,128)(2,1)S(1)}, u32[]{:S(2)}, u32[]{:S(2)}) %collective-permute-start.1) | collective-permute-done | bytes 1048608 | tf_op jit(solution)/shard_map/ppermute | solution.py:92
  26.8 16.0 %collective-permute-done.2 = bf16[128,4096]{1,0:T(8,128)(2,1)S(1)} collective-permute-done((bf16[128,4096]{1,0:T(8,128)(2,1)S(1)}, bf16[128,4096]{1,0:T(8,128)(2,1)S(1)}, u32[]{:S(2)}, u32[]{:S(2)}) %collective-permute-start.2) | collective-permute-done | bytes 1048608 | tf_op jit(solution)/shard_map/ppermute | solution.py:92
  43.8 16.0 %collective-permute-done.3 = bf16[128,4096]{1,0:T(8,128)(2,1)S(1)} collective-permute-done((bf16[128,4096]{1,0:T(8,128)(2,1)S(1)}, bf16[128,4096]{1,0:T(8,128)(2,1)S(1)}, u32[]{:S(2)}, u32[]{:S(2)}) %collective-permute-start.3) | collective-permute-done | bytes 1048608 | tf_op jit(solution)/shard_map/ppermute | solution.py:92
  60.8 16.0 %collective-permute-done.4 = bf16[128,4096]{1,0:T(8,128)(2,1)S(1)} collective-permute-done((bf16[128,4096]{1,0:T(8,128)(2,1)S(1)}, bf16[128,4096]{1,0:T(8,128)(2,1)S(1)}, u32[]{:S(2)}, u32[]{:S(2)}) %collective-permute-start.4) | collective-permute-done | bytes 1048608 | tf_op jit(solution)/shard_map/ppermute | solution.py:92
  77.8 16.1 %collective-permute-done.5 = bf16[128,4096]{1,0:T(8,128)(2,1)} collective-permute-done((bf16[128,4096]{1,0:T(8,128)(2,1)S(1)}, bf16[128,4096]{1,0:T(8,128)(2,1)}, u32[]{:S(2)}, u32[]{:S(2)}) %collective-permute-start.5) | collective-permute-done | bytes 1048608 | tf_op jit(solution)/shard_map/ppermute | solution.py:92
  97.2 13.0 %collective-permute-done.6 = bf16[128,4096]{1,0:T(8,128)(2,1)} collective-permute-done((bf16[128,4096]{1,0:T(8,128)(2,1)}, bf16[128,4096]{1,0:T(8,128)(2,1)}, u32[]{:S(2)}, u32[]{:S(2)}) %collective-permute-start.6) | collective-permute-done | bytes 1048608 | tf_op jit(solution)/shard_map/ppermute | solution.py:92
  112.2 4.9 %copy.92 = bf16[512,8,2,256]{3,1,2,0:T(8,128)(2,1)} copy(bf16[512,8,2,256]{3,2,1,0:T(2,128)(2,1)} %bitcast.87) | data formatting | bytes 8388608
  119.2 7.4 %collective-permute-done.7 = bf16[128,4096]{1,0:T(8,128)(2,1)} collective-permute-done((bf16[128,4096]{1,0:T(8,128)(2,1)}, bf16[128,4096]{1,0:T(8,128)(2,1)}, u32[]{:S(2)}, u32[]{:S(2)}) %collective-permute-start.7) | collective-permute-done | bytes 1048608 | tf_op jit(solution)/shard_map/ppermute | solution.py:92
  137.3 5.7 %copy-done.6 = bf16[2048,4096]{1,0:T(8,128)(2,1)} copy-done((bf16[2048,4096]{1,0:T(8,128)(2,1)}, bf16[2048,4096]{1,0:T(8,128)(2,1)S(1)}, u32[]{:S(2)}) %copy-start.6) | copy-done | bytes 16777240
  143.0 2.3 negate_multiply_fusion
  145.4 4.8 %reduce-window.14 = f32[4,4,2,128]{3,2,1,0:T(2,128)S(1)} reduce-window(f32[4,4,2,128]{3,2,1,0:T(2,128)S(1)} %copy.83, f32[]{:T(128)} %constant.109.clone.1), window={size=1x1x1x128 pad=0_0x0_0x0_0x127_0}, to_apply=%region_1.2 | reduce-window | flops 520192 | bytes 32772 | tf_op jit(solution)/shard_map/reduce-window
  151.0 8.3 %fusion.10 = f32[1024,512]{0,1:T(8,128)S(1)} fusion(bf16[4096,512]{1,0:T(8,128)(2,1)} %bitcast.88, bf16[2048,4096]{1,0:T(8,128)(2,1)} %copy-done.6, s32[]{:T(128)S(6)} %select_n.93), kind=kOutput, calls=%fused_computation.16 | convolution fusion | flops 4294967296 | bytes 14680068 | tf_op jit(solution)/shard_map/dot_general | solution.py:97
  159.4 7.3 %fusion.6 = f32[1024,128]{0,1:T(8,128)S(1)} fusion(bf16[2048,4096]{1,0:T(8,128)(2,1)} %copy-done.6, s32[]{:T(128)S(6)} %select_n.93, bf16[4096,128]{1,0:T(8,128)(2,1)} %collective-permute-done.8, bf16[4096,128]{1,0:T(8,128)(2,1)S(1)} %copy-done.29, pred[]{:T(512)S(6)} %eq.62), kind=kOutput, calls=%fused_computation.12 | convolution fusion | flops 1074266112 | bytes 11010053 | tf_op jit(solution)/shard_map/dot_general | solution.py:97
  166.7 6.3 %fusion.8 = f32[1024,128]{0,1:T(8,128)S(1)} fusion(bf16[2048,4096]{1,0:T(8,128)(2,1)} %copy-done.6, s32[]{:T(128)S(6)} %select_n.93, bf16[4096,128]{1,0:T(8,128)(2,1)S(1)} %copy-done.29, bf16[4096,128]{1,0:T(8,128)(2,1)} %collective-permute-done.8, pred[]{:T(512)S(6)} %eq.62), kind=kOutput, calls=%fused_computation.14 | convolution fusion | flops 1074266112 | bytes 11010053 | tf_op jit(solution)/shard_map/dot_general | solution.py:97
  173.1 4.1 collective-permute-start.9
  178.7 2.1 collective-permute-done.9
  180.9 2.3 divide_multiply_fusion
  186.0 2.7 reshape.145
  188.6 2.1 reshape.150
  190.7 3.4 fusion.47
  194.1 11.6 %while.31 = (s32[]{:T(128)}, f32[4,64,128]{2,1,0:T(8,128)S(1)}, f32[4]{0:T(128)S(1)}, f32[4,4,64,128]{3,2,1,0:T(8,128)}, f32[4,4]{1,0:T(4,128)}, /*index=5*/f32[...) while((s32[]{:T(128)}, f32[4,64,128]{2,1,0:T(8,128)S(1)}, f32[4]{0:T(128)S(1)}, ...), condition=%wide.region_7.8_spmd.clone, body=%wide.region_6.7_spmd.clone.sunk | while | flops 131083 | bytes 656117 | solution.py:150
  206.4 12.6 %all-gather.1 = f32[16,64,128]{2,1,0:T(8,128)} all-gather(f32[4,64,128]{2,1,0:T(8,128)S(1)} %get-tuple-element.142), channel_id=3, replica_groups=mesh['seq'=4,'tp'=8] {'seq'}, dimensions={0}, use_global_device_ids=true | all-gather | bytes 655360 | tf_op jit(solution)/shard_map/all_gather | solution.py:29
  219.0 9.6 %all-reduce.1 = f32[16]{0:T(128)} all-reduce(f32[16]{0:T(128)} %copy-done.31), channel_id=2, replica_groups=mesh['seq'=4,'tp'=8] {'seq'}, use_global_device_ids=true, to_apply=%add.1 | all-reduce | flops 16 | bytes 128
  229.9 6.8 %while.32 = (s32[]{:T(128)}, f32[4,64,128]{2,1,0:T(8,128)S(1)}, s32[]{:T(128)}, f32[4,4]{1,0:T(4,128)}, f32[4,4,64,128]{3,2,1,0:T(8,128)}, /*index=5*/s32[]{:T(128)}, s32[]{:T(128)}) while((s32[]{:T(128)}, f32[4,64,128]{2,1,0:T(8,128)S(1)}, s32[]{:T(128)}, f32[4,4]{1,0:T(4,128)}, f32[4,4,64,128]{3,2,1,0:T(8,128)}, ...), condition=%wide.region_9.10_spmd.clone, body=%wide.region_8.9_spmd.clone.sunk | while | flops 131076 | bytes 393369 | solution.py:38
  236.7 2.1 reshape.149
  238.8 2.2 fusion.56
  241.0 6.6 %fusion.41 = f32[4,256,4,64]{1,3,2,0:T(8,128)S(1)} fusion(f32[4,4,256]{2,1,0:T(4,128)} %copy.69, f32[4,256,256]{2,1,0:T(8,128)S(1)} %fusion.56, f32[4,4,256]{2,1,0:T(4,128)S(1)} %reduce_window_sum.41, pred[4,256,256]{2,1,0:T(8,128)(4,1)S(1)} %copy-done.17, f32[4,256,4,64]{1,0,3,2:T(4,128)} %reshape.145), kind=kOutput, calls=%fused_computation.59 | convolution fusion | flops 810549248 | bytes 3440640 | tf_op jit(solution)/shard_map/chij,cjhp->cihp/dot_general | solution.py:133
  251.5 8.2 %fusion.55 = f32[1024,4096]{1,0:T(8,128)} fusion(bf16[256,4096]{1,0:T(8,128)(2,1)S(1)} %copy-done, f32[1024,256]{0,1:T(8,128)S(1)} %get-tuple-element.213, f32[256]{0:T(256)S(1)} %copy-done.21, f32[1024]{0:T(1024)S(1)} %add_rsqrt_fusion), kind=kOutput, calls=%fused_computation.73 | convolution fusion | flops 2148270080 | bytes 19928064 | tf_op jit(solution)/shard_map/dot_general | solution.py:167
  259.8 164.8 %reduce-scatter.2.cloned.1.call-done = f32[128,4096]{1,0:T(8,128)} async-done(((f32[1024,4096]{1,0:T(8,128)}), f32[128,4096]{1,0:T(8,128)}) %reduce-scatter.2.cloned.1.call-update) | async-done | bytes 2097168 | tf_op jit(solution)/shard_map/reduce_scatter | solution.py:168
  424.5 2.8 fusion.31
  (176 shorter events, 49.8 us)
Async XLA Ops:
  6.5 245.0 %copy-start = (bf16[256,4096]{1,0:T(8,128)(2,1)S(1)}, bf16[256,4096]{1,0:T(8,128)(2,1)}, u32[]{:S(2)}) copy-start(bf16[256,4096]{1,0:T(8,128)(2,1)} %param.28) | copy-start | bytes 6291460
  6.5 418.0 %reduce-scatter.2.cloned.1.call-start = ((), (), s32[]{:S(2)}) async-start(), calls=%async_computation.1 | async-start | bytes 18874368 | tf_op jit(solution)/shard_map/reduce_scatter | solution.py:168
  9.8 17.0 %collective-permute-start.1 = (bf16[128,4096]{1,0:T(8,128)(2,1)S(1)}, bf16[128,4096]{1,0:T(8,128)(2,1)S(1)}, u32[]{:S(2)}, u32[]{:S(2)}) collective-permute-start(bf16[128,4096]{1,0:T(8,128)(2,1)S(1)} %fusion.30), channel_id=1, source_target_pairs={{0,1},{1,2},{2,3},{3,4},{4,5},{5,6},{6,7},{7,0},{8,9},{9,10},{10,1... | collective-permute-start | bytes 3145736 | tf_op jit(solution)/shard_map/ppermute | solution.py:92
  26.8 83.6 %copy-start.7 = (bf16[128,4096]{1,0:T(8,128)(2,1)}, bf16[128,4096]{1,0:T(8,128)(2,1)S(1)}, u32[]{:S(2)}) copy-start(bf16[128,4096]{1,0:T(8,128)(2,1)S(1)} %collective-permute-done.1) | copy-start | bytes 3145732
  26.8 16.0 %collective-permute-start.2 = (bf16[128,4096]{1,0:T(8,128)(2,1)S(1)}, bf16[128,4096]{1,0:T(8,128)(2,1)S(1)}, u32[]{:S(2)}, u32[]{:S(2)}) collective-permute-start(bf16[128,4096]{1,0:T(8,128)(2,1)S(1)} %collective-permute-done.1), channel_id=1, source_target_pairs={{0,1},{1,2},{2,3},{3,4},{4,5},{5,6},{6,7},{7,0},{8,9},{9,10},{10,1... | collective-permute-start | bytes 3145736 | tf_op jit(solution)/shard_map/ppermute | solution.py:92
  43.8 16.0 %collective-permute-start.3 = (bf16[128,4096]{1,0:T(8,128)(2,1)S(1)}, bf16[128,4096]{1,0:T(8,128)(2,1)S(1)}, u32[]{:S(2)}, u32[]{:S(2)}) collective-permute-start(bf16[128,4096]{1,0:T(8,128)(2,1)S(1)} %collective-permute-done.2), channel_id=1, source_target_pairs={{0,1},{1,2},{2,3},{3,4},{4,5},{5,6},{6,7},{7,0},{8,9},{9,10},{10,1... | collective-permute-start | bytes 3145736 | tf_op jit(solution)/shard_map/ppermute | solution.py:92
  60.8 16.0 %collective-permute-start.4 = (bf16[128,4096]{1,0:T(8,128)(2,1)S(1)}, bf16[128,4096]{1,0:T(8,128)(2,1)S(1)}, u32[]{:S(2)}, u32[]{:S(2)}) collective-permute-start(bf16[128,4096]{1,0:T(8,128)(2,1)S(1)} %collective-permute-done.3), channel_id=1, source_target_pairs={{0,1},{1,2},{2,3},{3,4},{4,5},{5,6},{6,7},{7,0},{8,9},{9,10},{10,1... | collective-permute-start | bytes 3145736 | tf_op jit(solution)/shard_map/ppermute | solution.py:92
  77.8 16.1 %collective-permute-start.5 = (bf16[128,4096]{1,0:T(8,128)(2,1)S(1)}, bf16[128,4096]{1,0:T(8,128)(2,1)}, u32[]{:S(2)}, u32[]{:S(2)}) collective-permute-start(bf16[128,4096]{1,0:T(8,128)(2,1)S(1)} %collective-permute-done.4), channel_id=1, source_target_pairs={{0,1},{1,2},{2,3},{3,4},{4,5},{5,6},{6,7},{7,0},{8,9},{9,10},{10,1... | collective-permute-start | bytes 3145736 | tf_op jit(solution)/shard_map/ppermute | solution.py:92
  93.9 16.3 %collective-permute-start.6 = (bf16[128,4096]{1,0:T(8,128)(2,1)}, bf16[128,4096]{1,0:T(8,128)(2,1)}, u32[]{:S(2)}, u32[]{:S(2)}) collective-permute-start(bf16[128,4096]{1,0:T(8,128)(2,1)} %collective-permute-done.5), channel_id=1, source_target_pairs={{0,1},{1,2},{2,3},{3,4},{4,5},{5,6},{6,7},{7,0},{8,9},{9,10},{10,1... | collective-permute-start | bytes 3145736 | tf_op jit(solution)/shard_map/ppermute | solution.py:92
  93.9 65.4 %collective-permute-start.8 = (bf16[4096,128]{1,0:T(8,128)(2,1)}, bf16[4096,128]{1,0:T(8,128)(2,1)}, u32[]{:S(2)}, u32[]{:S(2)}) collective-permute-start(bf16[4096,128]{1,0:T(8,128)(2,1)} %param.20), channel_id=1, source_target_pairs={{0,1},{1,0},{2,3},{3,2},{4,5},{5,4},{6,7},{7,6},{8,9},{9,8},{10,11... | collective-permute-start | bytes 3145736 | tf_op jit(solution)/shard_map/ppermute | solution.py:18
  93.9 25.1 %collective-permute-start = (bf16[4,128]{1,0:T(4,128)(2,1)}, bf16[4,128]{1,0:T(4,128)(2,1)S(1)}, u32[]{:S(2)}, u32[]{:S(2)}) collective-permute-start(bf16[4,128]{1,0:T(4,128)(2,1)} %param.25), channel_id=1, source_target_pairs={{0,1},{1,0},{2,3},{3,2},{4,5},{5,4},{6,7},{7,6},{8,9},{9,8},{10,11... | collective-permute-start | bytes 3080 | tf_op jit(solution)/shard_map/ppermute | solution.py:18
  110.3 16.3 %collective-permute-start.7 = (bf16[128,4096]{1,0:T(8,128)(2,1)}, bf16[128,4096]{1,0:T(8,128)(2,1)}, u32[]{:S(2)}, u32[]{:S(2)}) collective-permute-start(bf16[128,4096]{1,0:T(8,128)(2,1)} %collective-permute-done.6), channel_id=1, source_target_pairs={{0,1},{1,2},{2,3},{3,4},{4,5},{5,6},{6,7},{7,0},{8,9},{9,10},{10,1... | collective-permute-start | bytes 3145736 | tf_op jit(solution)/shard_map/ppermute | solution.py:92
  112.2 4.9 %copy-start.28 = (f32[4]{0:T(128)S(1)}, f32[4]{0:T(128)}, u32[]{:S(2)}) copy-start(f32[4]{0:T(128)} %param.26) | copy-start | bytes 52
  112.2 5.6 %copy-start.30 = (u32[32]{0:T(128)S(1)}, u32[32]{0:T(128)}, u32[]{:S(2)}) copy-start(u32[32]{0:T(128)} %constant.130) | copy-start | bytes 388
  112.2 6.9 %copy-start.27 = (bf16[4,128]{1,0:T(4,128)(2,1)S(1)}, bf16[4,128]{1,0:T(4,128)(2,1)}, u32[]{:S(2)}) copy-start(bf16[4,128]{1,0:T(4,128)(2,1)} %param.25) | copy-start | bytes 3076
  112.2 6.9 %copy-start.25 = (bf16[4,256]{1,0:T(4,128)(2,1)S(1)}, bf16[4,256]{1,0:T(4,128)(2,1)}, u32[]{:S(2)}) copy-start(bf16[4,256]{1,0:T(4,128)(2,1)} %param.24) | copy-start | bytes 6148
  119.2 13.0 %copy-start.12 = (bf16[128,4096]{1,0:T(8,128)(2,1)S(1)}, bf16[128,4096]{1,0:T(8,128)(2,1)}, u32[]{:S(2)}) copy-start(bf16[128,4096]{1,0:T(8,128)(2,1)} %copy-done.11) | copy-start | bytes 3145732
  127.9 4.3 copy-start.10
  132.4 4.2 copy-start.14
  136.7 6.3 %copy-start.20 = (bf16[4096,4]{0,1:T(4,128)(2,1)S(1)}, bf16[4096,4]{0,1:T(4,128)(2,1)}, u32[]{:S(2)}) copy-start(bf16[4096,4]{0,1:T(4,128)(2,1)} %param.21) | copy-start | bytes 98308
  136.7 6.3 %copy-start.23 = (f32[4]{0:T(128)S(1)}, f32[4]{0:T(128)}, u32[]{:S(2)}) copy-start(f32[4]{0:T(128)} %param.23) | copy-start | bytes 52
  136.7 6.3 %copy-start.24 = (f32[4]{0:T(128)S(1)}, f32[4]{0:T(128)}, u32[]{:S(2)}) copy-start(f32[4]{0:T(128)} %param.22) | copy-start | bytes 52
  137.3 5.7 %copy-start.6 = (bf16[2048,4096]{1,0:T(8,128)(2,1)}, bf16[2048,4096]{1,0:T(8,128)(2,1)S(1)}, u32[]{:S(2)}) copy-start(bf16[2048,4096]{1,0:T(8,128)(2,1)S(1)} %constant_dynamic-update-slice_fusion) | copy-start | bytes 50331652
  151.0 8.4 %copy-start.29 = (bf16[4096,128]{1,0:T(8,128)(2,1)S(1)}, bf16[4096,128]{1,0:T(8,128)(2,1)}, u32[]{:S(2)}) copy-start(bf16[4096,128]{1,0:T(8,128)(2,1)} %param.20) | copy-start | bytes 3145732
  159.4 18.6 %copy-start.4 = (f32[1024,512]{0,1:T(8,128)}, f32[1024,512]{0,1:T(8,128)S(1)}, u32[]{:S(2)}) copy-start(f32[1024,512]{0,1:T(8,128)S(1)} %fusion.10) | copy-start | bytes 6291460
  173.1 7.8 %collective-permute-start.9 = (f32[3,512]{0,1:T(8,128)S(1)}, f32[3,512]{0,1:T(8,128)S(1)}, u32[]{:S(2)}, u32[]{:S(2)}) collective-permute-start(f32[3,512]{0,1:T(8,128)S(1)} %pad_maximum_fusion.3), channel_id=1, source_target_pairs={{0,8},{8,16},{16,24},{1,9},{9,17},{17,25},{2,10},{10,18},{18,26},{... | collective-permute-start | bytes 18440 | tf_op jit(solution)/shard_map/ppermute | solution.py:24
  219.0 22.0 %copy-start.17 = (pred[4,256,256]{2,1,0:T(8,128)(4,1)S(1)}, pred[4,256,256]{2,1,0:T(8,128)(4,1)}, u32[]{:S(2)}) copy-start(pred[4,256,256]{2,1,0:T(8,128)(4,1)} %compare_and_fusion) | copy-start | bytes 786436
  241.0 6.7 %copy-start.15 = (f32[4,256,128]{1,0,2:T(4,128)S(1)}, f32[4,256,128]{1,0,2:T(4,128)}, u32[]{:S(2)}) copy-start(f32[4,256,128]{1,0,2:T(4,128)} %reshape.149) | copy-start | bytes 1572868
  241.0 6.7 %copy-start.16 = (f32[4,4,64,128]{3,2,1,0:T(8,128)S(1)}, f32[4,4,64,128]{3,2,1,0:T(8,128)}, u32[]{:S(2)}) copy-start(f32[4,4,64,128]{3,2,1,0:T(8,128)} %get-tuple-element.139) | copy-start | bytes 1572868
  241.0 6.7 %copy-start.19 = (f32[4,256,4]{1,2,0:T(4,128)S(1)}, f32[4,256,4]{1,2,0:T(4,128)}, u32[]{:S(2)}) copy-start(f32[4,256,4]{1,2,0:T(4,128)} %multiply_bitcast_fusion) | copy-start | bytes 49156
  241.0 6.7 %copy-start.26 = (f32[4,4]{1,0:T(4,128)S(1)}, f32[4,4]{1,0:T(4,128)}, u32[]{:S(2)}) copy-start(f32[4,4]{1,0:T(4,128)} %get-tuple-element.140) | copy-start | bytes 196
  250.3 1.2 collective-permute-start.10
  (12 other events, 20.7 us)
Sparse Core Ops, SparseCore 0:
  259.9 164.6 reduce-scatter.1
